TPU v7x, 32 devices: a whole 2x2x4 slice. The times are simulated.
32 devices in a mesh: groups: 2 (over y), tok: 4 (over z), slot: 2 (over x), hid: 2 (over core).
Axes of the slice: x: 2, y: 2, z: 4, core: 2. Of those that a mesh axis runs over, the one named last changes fastest.
Arguments:
- tokens: bfloat16 [8192, 1024], P(('groups', 'tok', 'slot', 'hid')), parts along dimension 0, may hold values from -12 to 12
- slot_keys: bfloat16 [2048, 512], P('groups', 'slot'), parts along dimension 0, may hold values from -12 to 12
- w_in: bfloat16 [4, 4, 1024, 4096], P(('groups', 'slot'), 'tok', None, 'hid'), parts along dimension 0, may hold values from -0.1875 to 0.1875
- w_out: bfloat16 [4, 4, 4096, 1024], P(('groups', 'slot'), 'tok', 'hid'), parts along dimension 0, may hold values from -0.09375 to 0.09375
Outputs:
- mixed: float32 [8192, 1024], P(('groups', 'tok', 'slot', 'hid')), parts along dimension 0
There are 2 independent parts, one for each index of `groups`. A program takes and returns all parts, laid end to end along the dimension named above; each array names one. Nothing has to cross between parts.
All inputs are finite; a program needn't handle non-finite values.
Results may differ from a plain program's by a relative error of at most 0.0022.
Values may be sent and summed in bfloat16 or wider, within the bound.
No kernel may reach another device: no remote copies, remote signals or barrier semaphores. Data moves between devices by JAX's collectives and lax.ppermute only.
A program may use at most 64 MiB of HBM per device.

v0:
```python
import jax
import jax.numpy as jnp
from jax import lax
from jax.sharding import PartitionSpec as P

epsilon = 1e-06


def local(tokens, slot_keys, w_in, w_out):
    model_width = tokens.shape[1]
    block_width = slot_keys.shape[1]
    owned_slots = block_width // (lax.axis_size("tok") * lax.axis_size("hid"))
    key_scale = lax.rsqrt(jnp.mean(jnp.square(slot_keys.astype(jnp.float32)), axis=0) + epsilon)
    fragment = lax.all_gather(tokens, "slot", axis=0, tiled=True)
    token_scale = lax.rsqrt(jnp.mean(jnp.square(fragment.astype(jnp.float32)), axis=1) + epsilon)
    logits = (
        4.0
        * token_scale[:, None]
        * key_scale[None, :]
        * jnp.dot(fragment, slot_keys, preferred_element_type=jnp.float32)
        / model_width
    )
    weights_exp = jnp.exp(logits)
    weights_low = weights_exp.astype(jnp.bfloat16)
    slot_numer = lax.dot_general(
        weights_low, fragment, (((0,), (0,)), ((), ())), preferred_element_type=jnp.float32
    )
    slot_denom = jnp.sum(weights_exp, axis=0)
    weights_all = weights_low
    token_denom = jnp.sum(weights_exp, axis=1)
    slot_numer, slot_denom, weights_all, token_denom = (
        slot_numer,
        slot_denom,
        weights_all,
        token_denom,
    )
    summed_numer, summed_denom = lax.psum((slot_numer, slot_denom), ("tok", "hid"))
    first_slot = lax.axis_index(("tok", "hid")) * owned_slots
    owned_numer = lax.dynamic_slice_in_dim(summed_numer, first_slot, owned_slots, 0)
    owned_denom = lax.dynamic_slice_in_dim(summed_denom, first_slot, owned_slots, 0)
    owned_inputs = (owned_numer / owned_denom[:, None]).astype(jnp.bfloat16)
    expert_inputs = lax.all_gather(owned_inputs, "hid", axis=0, tiled=True)
    hidden = jax.nn.gelu(
        jnp.dot(expert_inputs, w_in[0, 0], preferred_element_type=jnp.float32), approximate=True
    ).astype(jnp.bfloat16)
    half_outputs = jnp.dot(hidden, w_out[0, 0], preferred_element_type=jnp.float32)
    owned_outputs = lax.psum_scatter(half_outputs, "hid", scatter_dimension=0, tiled=True).astype(
        jnp.bfloat16
    )
    block_outputs = lax.all_gather(owned_outputs, ("tok", "hid"), axis=0, tiled=True)
    token_numer = jnp.dot(weights_all, block_outputs, preferred_element_type=jnp.float32)
    mine_numer, mine_denom = (
        lax.psum_scatter(token_numer, "slot", scatter_dimension=0, tiled=True),
        lax.psum_scatter(token_denom, "slot", scatter_dimension=0, tiled=True),
    )
    return mine_numer / mine_denom[:, None]


def solution(mesh):
    in_specs = (
        P(("groups", "tok", "slot", "hid"), None),
        P("groups", "slot"),
        P(("groups", "slot"), "tok", None, "hid"),
        P(("groups", "slot"), "tok", "hid", None),
    )
    out_specs = P(("groups", "tok", "slot", "hid"), None)
    return jax.shard_map(local, mesh=mesh, in_specs=in_specs, out_specs=out_specs, check_vma=False)
```

profile of v0, /device:TPU:0, one launch (start us, length us, event | category | flops | bytes accessed | tf_op | source)
XLA Modules:
  0.0 172.2 jit_solution(18349934714928174129)
XLA Ops:
  6.5 0.0 all-gather.2.cloned.1.call-start
  6.5 0.7 all-gather.2.cloned.1.call-update
  7.3 0.0 all-reduce.3.cloned.1.call-start
  7.3 1.2 multiply_reduce_fusion.1
  8.5 24.4 %all-gather.2.cloned.1.call-done = bf16[512,1024]{1,0:T(8,128)(2,1)} async-done(((bf16[256,1024]{1,0:T(8,128)(2,1)}), bf16[512,1024]{1,0:T(8,128)(2,1)}) %all-gather.2.cloned.1.call-update) | async-done | bytes 1048592 | tf_op jit(solution)/shard_map/all_gather | solution.py:14
  32.9 0.0 copy-start
  32.9 1.6 multiply_reduce_fusion
  34.5 1.9 %fusion.32 = (f32[512]{0:T(512)S(1)}, f32[256]{0:T(256)S(1)}, bf16[512,256]{1,0:T(8,128)(2,1)S(1)}) fusion(bf16[512,1024]{1,0:T(8,128)(2,1)} %all-gather.2.cloned.1.call-done, bf16[1024,256]{1,0:T(8,128)(2,1)} %param.5, f32[256]{0:T(256)S(1)} %add_rsqrt_fusion, f32[512]{0:T(512)S(1)} %rsqrt_multiply_fusion), kind=kOutput, calls=%fused_computation.34 | convolution fusion | flops 269221120 | bytes 1841152 | tf_op jit(solution)/shard_map/dot_general | solution.py:20
  36.4 0.0 copy-done
  36.4 1.4 fusion.26
  37.9 0.0 all-reduce.3.cloned.1.call-update
  37.9 0.0 reduce-scatter.3.cloned.1.call-start
  38.0 16.4 %psum.15 = f32[256]{0:T(256)S(1)} all-reduce(f32[256]{0:T(256)S(1)} %get-tuple-element.6), channel_id=1, replica_groups=mesh['groups'=2,'tok'=4,'slot'=2,'hid'=2] {'tok','hid'}, use_global_device_ids=true, to_apply=%region_4.0 | all-reduce | flops 256 | bytes 2048 | tf_op jit(solution)/shard_map/psum | solution.py:37
  54.4 0.1 dynamic_slice.7
  54.5 42.5 %all-reduce.3.cloned.1.call-done = f32[256,1024]{1,0:T(8,128)} async-done(((f32[256,1024]{1,0:T(8,128)}), f32[256,1024]{1,0:T(8,128)}) %all-reduce.3.cloned.1.call-update) | async-done | bytes 1048592 | tf_op jit(solution)/shard_map/psum | solution.py:37
  97.0 1.0 divide_convert_fusion
  98.0 1.9 %all_gather.10 = bf16[64,1024]{1,0:T(8,128)(2,1)S(1)} all-gather(bf16[32,1024]{1,0:T(8,128)(2,1)S(1)} %divide_convert_fusion), channel_id=1, replica_groups=mesh['groups'=2,'tok'=4,'slot'=2,'hid'=2] {'hid'}, dimensions={0}, use_global_device_ids=true | all-gather | bytes 196608 | tf_op jit(solution)/shard_map/all_gather | solution.py:42
  99.9 5.9 %fusion = f32[64,1024]{1,0:T(8,128)} fusion(bf16[1,1,2048,1024]{3,2,1,0:T(8,128)(2,1)} %param.7, bf16[64,1024]{1,0:T(8,128)(2,1)S(1)} %all_gather.10, bf16[1,1,1024,2048]{3,2,1,0:T(8,128)(2,1)} %param.6), kind=kOutput, calls=%fused_computation | convolution fusion | flops 538050560 | bytes 8781824 | tf_op jit(solution)/shard_map/dot_general | solution.py:46
  105.7 0.0 copy-start.1
  105.7 0.0 reduce-scatter.3.cloned.1.call-update
  105.7 0.0 reduce-scatter.5.cloned.1.call-start
  105.8 6.7 %reduce-scatter.3.cloned.1.call-done = f32[32,1024]{1,0:T(8,128)} async-done(((f32[64,1024]{1,0:T(8,128)}), f32[32,1024]{1,0:T(8,128)}) %reduce-scatter.3.cloned.1.call-update) | async-done | bytes 131088 | tf_op jit(solution)/shard_map/reduce_scatter | solution.py:47
  112.5 0.9 convert_element_type.23
  113.4 15.0 %all_gather.11 = bf16[256,1024]{1,0:T(8,128)(2,1)S(1)} all-gather(bf16[32,1024]{1,0:T(8,128)(2,1)S(1)} %convert_element_type.23), channel_id=1, replica_groups=mesh['groups'=2,'tok'=4,'slot'=2,'hid'=2] {'tok','hid'}, dimensions={0}, use_global_device_ids=true | all-gather | bytes 589824 | tf_op jit(solution)/shard_map/all_gather | solution.py:50
  128.4 1.8 %fusion.24 = f32[512,1024]{1,0:T(8,128)} fusion(bf16[256,1024]{1,0:T(8,128)(2,1)S(1)} %all_gather.11, bf16[512,256]{1,0:T(8,128)(2,1)S(1)} %get-tuple-element.7), kind=kOutput, calls=%fused_computation.24 | convolution fusion | flops 268435456 | bytes 2883584 | tf_op jit(solution)/shard_map/dot_general | solution.py:51
  130.2 0.0 reduce-scatter.5.cloned.1.call-update
  130.2 0.0 copy-done.1
  130.3 0.6 dynamic-slice
  131.5 4.9 %all-reduce = f32[512]{0:T(512)S(1)} all-reduce(f32[512]{0:T(512)S(1)} %get-tuple-element.5), channel_id=4, replica_groups=mesh['groups'=2,'tok'=4,'slot'=2,'hid'=2] {'slot'}, use_global_device_ids=true, to_apply=%region_8.0.clone | all-reduce | flops 512 | bytes 4096
  136.4 0.1 dynamic-slice.1
  136.5 26.8 %reduce-scatter.5.cloned.1.call-done = f32[256,1024]{1,0:T(8,128)} async-done(((f32[512,1024]{1,0:T(8,128)}), f32[256,1024]{1,0:T(8,128)}) %reduce-scatter.5.cloned.1.call-update) | async-done | bytes 1048592 | tf_op jit(solution)/shard_map/reduce_scatter | solution.py:53
  163.3 2.3 %broadcast_divide_fusion = f32[256,1024]{1,0:T(8,128)} fusion(f32[256,1024]{1,0:T(8,128)} %reduce-scatter.5.cloned.1.call-done, f32[256]{0:T(256)S(1)} %dynamic-slice.1), kind=kLoop, calls=%fused_computation.18 | loop fusion | flops 262144 | bytes 2098176 | tf_op jit(solution)/shard_map/div | solution.py:56
  (2 shorter events, 0.0 us)
Async XLA Ops:
  6.5 26.4 %all-gather.2.cloned.1.call-start = ((), (), s32[]{:S(2)}) async-start(), calls=%async_computation.2 | async-start | bytes 1572864 | tf_op jit(solution)/shard_map/all_gather | solution.py:14
  7.3 89.7 %all-reduce.3.cloned.1.call-start = ((), (), s32[]{:S(2)}) async-start(), calls=%async_computation.3 | async-start | bytes 2097152 | tf_op jit(solution)/shard_map/psum | solution.py:37
  32.9 3.5 %copy-start = (bf16[512,1024]{1,0:T(8,128)(2,1)S(1)}, bf16[512,1024]{1,0:T(8,128)(2,1)}, u32[]{:S(2)}) copy-start(bf16[512,1024]{1,0:T(8,128)(2,1)} %all-gather.2.cloned.1.call-done) | copy-start | bytes 3145732
  37.9 74.6 %reduce-scatter.3.cloned.1.call-start = ((), (), s32[]{:S(2)}) async-start(), calls=%async_computation.4 | async-start | bytes 393216 | tf_op jit(solution)/shard_map/reduce_scatter | solution.py:47
  105.7 24.5 %copy-start.1 = (u32[32]{0:T(128)S(1)}, u32[32]{0:T(128)}, u32[]{:S(2)}) copy-start(u32[32]{0:T(128)} %constant.43) | copy-start | bytes 388
  105.7 57.6 %reduce-scatter.5.cloned.1.call-start = ((), (), s32[]{:S(2)}) async-start(), calls=%async_computation.5 | async-start | bytes 3145728 | tf_op jit(solution)/shard_map/reduce_scatter | solution.py:53
Sparse Core Ops, SparseCore 0:
  8.9 23.9 all-gather.1
  38.0 58.8 all-reduce.2
  105.9 6.6 reduce-scatter.2
  130.4 32.8 reduce-scatter.4
where the time goes:
time: 173 us; the launch traced here: 172 us
  waiting for transfers between devices  101 us (58%)
  blocking collectives  38.2 us (22%)
  between operations  13.8 us (8%)
  matrix products  11 us (6%)
  other arithmetic  7.06 us (4%)
    psum x1, waiting for transfers between devices, local(): lax.psum((slot_numer, slot_denom), ('tok', 'hid'))  42.5 us
    reduce_scatter x1, waiting for transfers between devices, local(): lax.psum_scatter(token_numer, 'slot', scatter_dimension=0, tiled=True)  26.8 us
    all_gather x1, waiting for transfers between devices, local(): fragment = lax.all_gather(tokens, 'slot', axis=0, tiled=True)  24.4 us
    psum x1, blocking collectives, local(): lax.psum((slot_numer, slot_denom), ('tok', 'hid'))  16.4 us
    all_gather x1, blocking collectives, local(): lax.all_gather(owned_outputs, ('tok', 'hid'), axis=0, tiled=True)  15 us
    reduce_scatter x1, waiting for transfers between devices, local(): lax.psum_scatter(half_outputs, 'hid', scatter_dimension=0, tiled=True)  6.72 us
    dot_general x1, matrix products, local(): jnp.dot(hidden, w_out[0, 0], preferred_element_type=jnp.float32)  5.86 us
    unnamed x1, blocking collectives  4.94 us
  transfers between devices with their start and end apart: 4, of which 4 were waited for; matrix products, arithmetic and copies ran while one was open for 1% of the time, Pallas kernels for 0%

commit v1 on v0

--- a/solution.py
+++ b/solution.py
@@ -4,6 +4,12 @@
 from jax.sharding import PartitionSpec as P
 
 epsilon = 1e-06
+
+
+def _replace_ports(block_in, mesh_name, a_name):
+    for to_i in (mesh_name, a_name):
+        block_in = lax.psum(block_in, to_i)
+    return block_in
 
 
 def local(tokens, slot_keys, w_in, w_out):
@@ -34,7 +40,7 @@
         weights_all,
         token_denom,
     )
-    summed_numer, summed_denom = lax.psum((slot_numer, slot_denom), ("tok", "hid"))
+    summed_numer, summed_denom = _replace_ports((slot_numer, slot_denom), "hid", "tok")
     first_slot = lax.axis_index(("tok", "hid")) * owned_slots
     owned_numer = lax.dynamic_slice_in_dim(summed_numer, first_slot, owned_slots, 0)
     owned_denom = lax.dynamic_slice_in_dim(summed_denom, first_slot, owned_slots, 0)

time: 173 us -> 189 us (1.092)
  waiting for transfers between devices: 101 us -> 120 us
  blocking collectives: 38.2 us -> 36.2 us
    psum x1 -> x2, waiting for transfers between devices: 42.5 us -> 60.7 us  [_replace_ports(): block_in = lax.psum(block_in, to_i)]
    psum x1 -> x2, blocking collectives: 16.4 us -> 14.4 us  [_replace_ports(): block_in = lax.psum(block_in, to_i)]
  transfers between devices with their start and end apart: 4 -> 5, of which waited for: 4 -> 5; matrix products, arithmetic and copies ran while one was open for 1% -> 1% of each run, Pallas kernels for 0% -> 0%
where the time goes in v1:
time: 189 us
  waiting for transfers between devices  120 us (63%)
  blocking collectives  36.2 us (19%)
  between operations  13.8 us (7%)
  matrix products  11 us (6%)
  other arithmetic  7.06 us (4%)
    psum x2, waiting for transfers between devices, _replace_ports(): block_in = lax.psum(block_in, to_i)  60.7 us
    reduce_scatter x1, waiting for transfers between devices, local(): lax.psum_scatter(token_numer, 'slot', scatter_dimension=0, tiled=True)  26.8 us
    all_gather x1, waiting for transfers between devices, local(): fragment = lax.all_gather(tokens, 'slot', axis=0, tiled=True)  24.4 us
    all_gather x1, blocking collectives, local(): lax.all_gather(owned_outputs, ('tok', 'hid'), axis=0, tiled=True)  15 us
    psum x2, blocking collectives, _replace_ports(): block_in = lax.psum(block_in, to_i)  14.4 us
    reduce_scatter x1, waiting for transfers between devices, local(): lax.psum_scatter(half_outputs, 'hid', scatter_dimension=0, tiled=True)  7.14 us
    dot_general x1, matrix products, local(): jnp.dot(hidden, w_out[0, 0], preferred_element_type=jnp.float32)  5.87 us
    unnamed x1, blocking collectives  4.94 us
  transfers between devices with their start and end apart: 5, of which 5 were waited for; matrix products, arithmetic and copies ran while one was open for 1% of the time, Pallas kernels for 0%

profile of v1, /device:TPU:0, one launch (start us, length us, event | category | flops | bytes accessed | tf_op | source)
XLA Modules:
  0.0 188.9 jit_solution(5049426355244155863)
XLA Ops:
  6.5 0.0 all-gather.2.cloned.1.call-start
  6.5 0.7 all-gather.2.cloned.1.call-update
  7.3 0.0 all-reduce.4.cloned.1.call-start
  7.3 1.2 multiply_reduce_fusion.1
  8.5 24.4 %all-gather.2.cloned.1.call-done = bf16[512,1024]{1,0:T(8,128)(2,1)} async-done(((bf16[256,1024]{1,0:T(8,128)(2,1)}), bf16[512,1024]{1,0:T(8,128)(2,1)}) %all-gather.2.cloned.1.call-update) | async-done | bytes 1048592 | tf_op jit(solution)/shard_map/all_gather | solution.py:20
  32.9 0.0 copy-start
  32.9 1.6 multiply_reduce_fusion
  34.5 1.9 %fusion.32 = (f32[512]{0:T(512)S(1)}, f32[256]{0:T(256)S(1)}, bf16[512,256]{1,0:T(8,128)(2,1)S(1)}) fusion(bf16[512,1024]{1,0:T(8,128)(2,1)} %all-gather.2.cloned.1.call-done, bf16[1024,256]{1,0:T(8,128)(2,1)} %param.5, f32[256]{0:T(256)S(1)} %add_rsqrt_fusion, f32[512]{0:T(512)S(1)} %rsqrt_multiply_fusion), kind=kOutput, calls=%fused_computation.34 | convolution fusion | flops 269221120 | bytes 1841152 | tf_op jit(solution)/shard_map/dot_general | solution.py:26
  36.4 0.0 copy-done
  36.4 1.4 fusion.26
  37.9 0.0 all-reduce.4.cloned.1.call-update
  37.9 0.0 all-reduce.6.cloned.1.call-start
  38.0 19.7 %all-reduce.4.cloned.1.call-done = f32[256,1024]{1,0:T(8,128)} async-done(((f32[256,1024]{1,0:T(8,128)}), f32[256,1024]{1,0:T(8,128)}) %all-reduce.4.cloned.1.call-update) | async-done | bytes 1048592 | tf_op jit(solution)/shard_map/psum | solution.py:11
  57.7 0.0 all-reduce.6.cloned.1.call-update
  57.7 0.0 reduce-scatter.3.cloned.1.call-start
  57.7 2.5 %psum.30 = f32[256]{0:T(256)S(1)} all-reduce(f32[256]{0:T(256)S(1)} %get-tuple-element.6), channel_id=1, replica_groups=mesh['groups'=2,'tok'=4,'slot'=2,'hid'=2] {'hid'}, use_global_device_ids=true, to_apply=%region_5.0 | all-reduce | flops 256 | bytes 2048 | tf_op jit(solution)/shard_map/psum | solution.py:11
  60.2 11.9 %psum.31 = f32[256]{0:T(256)S(1)} all-reduce(f32[256]{0:T(256)S(1)} %psum.30), channel_id=1, replica_groups=mesh['groups'=2,'tok'=4,'slot'=2,'hid'=2] {'tok'}, use_global_device_ids=true, to_apply=%region_6.0 | all-reduce | flops 256 | bytes 2048 | tf_op jit(solution)/shard_map/psum | solution.py:11
  72.2 0.1 dynamic_slice.7
  72.2 41.0 %all-reduce.6.cloned.1.call-done = f32[256,1024]{1,0:T(8,128)} async-done(((f32[256,1024]{1,0:T(8,128)}), f32[256,1024]{1,0:T(8,128)}) %all-reduce.6.cloned.1.call-update) | async-done | bytes 1048592 | tf_op jit(solution)/shard_map/psum | solution.py:11
  113.2 1.0 divide_convert_fusion
  114.2 1.9 %all_gather.10 = bf16[64,1024]{1,0:T(8,128)(2,1)S(1)} all-gather(bf16[32,1024]{1,0:T(8,128)(2,1)S(1)} %divide_convert_fusion), channel_id=1, replica_groups=mesh['groups'=2,'tok'=4,'slot'=2,'hid'=2] {'hid'}, dimensions={0}, use_global_device_ids=true | all-gather | bytes 196608 | tf_op jit(solution)/shard_map/all_gather | solution.py:48
  116.1 5.9 %fusion = f32[64,1024]{1,0:T(8,128)} fusion(bf16[1,1,2048,1024]{3,2,1,0:T(8,128)(2,1)} %param.7, bf16[64,1024]{1,0:T(8,128)(2,1)S(1)} %all_gather.10, bf16[1,1,1024,2048]{3,2,1,0:T(8,128)(2,1)} %param.6), kind=kOutput, calls=%fused_computation | convolution fusion | flops 538050560 | bytes 8781824 | tf_op jit(solution)/shard_map/dot_general | solution.py:52
  122.0 0.0 copy-start.1
  122.0 0.0 reduce-scatter.3.cloned.1.call-update
  122.0 0.0 reduce-scatter.5.cloned.1.call-start
  122.1 7.1 %reduce-scatter.3.cloned.1.call-done = f32[32,1024]{1,0:T(8,128)} async-done(((f32[64,1024]{1,0:T(8,128)}), f32[32,1024]{1,0:T(8,128)}) %reduce-scatter.3.cloned.1.call-update) | async-done | bytes 131088 | tf_op jit(solution)/shard_map/reduce_scatter | solution.py:53
  129.2 0.9 convert_element_type.23
  130.1 15.0 %all_gather.11 = bf16[256,1024]{1,0:T(8,128)(2,1)S(1)} all-gather(bf16[32,1024]{1,0:T(8,128)(2,1)S(1)} %convert_element_type.23), channel_id=1, replica_groups=mesh['groups'=2,'tok'=4,'slot'=2,'hid'=2] {'tok','hid'}, dimensions={0}, use_global_device_ids=true | all-gather | bytes 589824 | tf_op jit(solution)/shard_map/all_gather | solution.py:56
  145.1 1.8 fusion.24
  146.9 0.0 reduce-scatter.5.cloned.1.call-update
  146.9 0.0 copy-done.1
  146.9 0.6 dynamic-slice
  148.2 4.9 %all-reduce = f32[512]{0:T(512)S(1)} all-reduce(f32[512]{0:T(512)S(1)} %get-tuple-element.5), channel_id=4, replica_groups=mesh['groups'=2,'tok'=4,'slot'=2,'hid'=2] {'slot'}, use_global_device_ids=true, to_apply=%region_10.0.clone | all-reduce | flops 512 | bytes 4096
  153.1 0.1 dynamic-slice.1
  153.2 26.8 %reduce-scatter.5.cloned.1.call-done = f32[256,1024]{1,0:T(8,128)} async-done(((f32[512,1024]{1,0:T(8,128)}), f32[256,1024]{1,0:T(8,128)}) %reduce-scatter.5.cloned.1.call-update) | async-done | bytes 1048592 | tf_op jit(solution)/shard_map/reduce_scatter | solution.py:59
  180.0 2.3 %broadcast_divide_fusion = f32[256,1024]{1,0:T(8,128)} fusion(f32[256,1024]{1,0:T(8,128)} %reduce-scatter.5.cloned.1.call-done, f32[256]{0:T(256)S(1)} %dynamic-slice.1), kind=kLoop, calls=%fused_computation.18 | loop fusion | flops 262144 | bytes 2098176 | tf_op jit(solution)/shard_map/div | solution.py:62
  (2 shorter events, 0.0 us)
Async XLA Ops:
  6.5 26.4 %all-gather.2.cloned.1.call-start = ((), (), s32[]{:S(2)}) async-start(), calls=%async_computation.2 | async-start | bytes 1572864 | tf_op jit(solution)/shard_map/all_gather | solution.py:20
  7.3 50.4 %all-reduce.4.cloned.1.call-start = ((), (), s32[]{:S(2)}) async-start(), calls=%async_computation.3 | async-start | bytes 2097152 | tf_op jit(solution)/shard_map/psum | solution.py:11
  32.9 3.5 %copy-start = (bf16[512,1024]{1,0:T(8,128)(2,1)S(1)}, bf16[512,1024]{1,0:T(8,128)(2,1)}, u32[]{:S(2)}) copy-start(bf16[512,1024]{1,0:T(8,128)(2,1)} %all-gather.2.cloned.1.call-done) | copy-start | bytes 3145732
  37.9 75.3 %all-reduce.6.cloned.1.call-start = ((), (), s32[]{:S(2)}) async-start(), calls=%async_computation.4 | async-start | bytes 2097152 | tf_op jit(solution)/shard_map/psum | solution.py:11
  57.7 71.5 %reduce-scatter.3.cloned.1.call-start = ((), (), s32[]{:S(2)}) async-start(), calls=%async_computation.5 | async-start | bytes 393216 | tf_op jit(solution)/shard_map/reduce_scatter | solution.py:53
  122.0 24.9 %copy-start.1 = (u32[32]{0:T(128)S(1)}, u32[32]{0:T(128)}, u32[]{:S(2)}) copy-start(u32[32]{0:T(128)} %constant.43) | copy-start | bytes 388
  122.0 58.0 %reduce-scatter.5.cloned.1.call-start = ((), (), s32[]{:S(2)}) async-start(), calls=%async_computation.6 | async-start | bytes 3145728 | tf_op jit(solution)/shard_map/reduce_scatter | solution.py:59
Sparse Core Ops, SparseCore 0:
  8.9 23.9 all-gather.1
  38.0 19.5 all-reduce.3
  60.2 53.0 all-reduce.5
  122.1 7.0 reduce-scatter.2
  147.1 32.9 reduce-scatter.4
